TPU v7x, 512 devices: a whole 4x4x16 slice. The times are simulated.
512 devices in a mesh: group: 16 (over z), shard: 32 (over y, x, core).
Axes of the slice: x: 4, y: 4, z: 16, core: 2. Of those that a mesh axis runs over, the one named last changes fastest.
Arguments:
- entry_grads: float32 [16, 32, 256, 1280], P('group', 'shard'), may hold values from -800 to 800
- exit_grads: float32 [16, 32, 256, 1024], P('group', 'shard'), may hold values from -800 to 800
- entry_params: float32 [32, 256, 1280], P('shard', 'group'), may hold values from -0.15625 to 0.15625
- exit_params: float32 [32, 256, 1024], P('shard', 'group'), may hold values from -0.15625 to 0.15625
- entry_mean: float32 [32, 256, 1280], P('shard', 'group'), may hold values from -1.5 to 1.5
- exit_mean: float32 [32, 256, 1024], P('shard', 'group'), may hold values from -1.5 to 1.5
- entry_square: float32 [32, 256, 1280], P('shard', 'group'), may hold values from 0.01 to 1
- exit_square: float32 [32, 256, 1024], P('shard', 'group'), may hold values from 0.01 to 1
Outputs:
- entry_master: float32 [32, 256, 1280], P('shard', 'group')
- exit_master: float32 [32, 256, 1024], P('shard', 'group')
- entry_moment: float32 [32, 256, 1280], P('shard', 'group')
- exit_moment: float32 [32, 256, 1024], P('shard', 'group')
- entry_variance: float32 [32, 256, 1280], P('shard', 'group')
- exit_variance: float32 [32, 256, 1024], P('shard', 'group')
- entry_weights: bfloat16 [32, 256, 1280], P('shard')
- exit_weights: bfloat16 [32, 256, 1024], P('shard')
All inputs are finite; a program needn't handle non-finite values.
Results may differ from a plain program's by a relative error of at most 0.0004.
Values may be sent and summed in bfloat16 or wider, within the bound.
No kernel may reach another device: no remote copies, remote signals or barrier semaphores. Data moves between devices by JAX's collectives and lax.ppermute only.
A program may use at most 64 MiB of HBM per device.

v0:
```python
import jax
import jax.numpy as jnp
from jax import lax
from jax.sharding import PartitionSpec as P

beta_first = 0.9
beta_second = 0.95
learn_rate = 0.01
decay_rate = 0.1
epsilon = 1e-08
correct_first = 1.0 - 0.9**40
correct_second = 1.0 - 0.95**40


def adamw_step(params, mean, square, total, clip):
    grads = clip * total
    moment = beta_first * mean + (1.0 - beta_first) * grads
    variance = beta_second * square + (1.0 - beta_second) * grads * grads
    update = moment / correct_first / (jnp.sqrt(variance / correct_second) + epsilon)
    master = params - learn_rate * (update + decay_rate * params)
    return (master, moment, variance)


def sum_everywhere(values):
    axes = ("group", "shard")
    lanes = jnp.sum(values.reshape(-1, 128), axis=0)
    sent = jnp.broadcast_to(lanes, (lax.axis_size(axes), 1, 128))
    return jnp.sum(lax.all_to_all(sent, axes, 0, 0))


def body(
    entry_grads,
    exit_grads,
    entry_params,
    exit_params,
    entry_mean,
    exit_mean,
    entry_square,
    exit_square,
):
    entry_rows_dev = entry_grads.shape[2]
    exit_rows_dev = exit_grads.shape[2]
    entry_width = entry_grads.shape[3]
    exit_width = exit_grads.shape[3]
    entry_local = entry_grads.reshape(entry_rows_dev, entry_width)
    exit_local = exit_grads.reshape(exit_rows_dev, exit_width)
    packed = jnp.concatenate([entry_local, exit_local], axis=1)
    total = lax.psum_scatter(packed, "group", scatter_dimension=0, tiled=True)
    entry_total = total[:, :entry_width]
    exit_total = total[:, entry_width:]
    squares = sum_everywhere(total * total)
    count = (entry_rows_dev * entry_width + exit_rows_dev * exit_width) * lax.axis_size("shard")
    limit = jnp.sqrt(jnp.float32(count))
    clip = jnp.minimum(jnp.float32(1.0), limit / (jnp.sqrt(squares) + 1e-06))
    entry_master, entry_moment, entry_variance = adamw_step(
        entry_params[0], entry_mean[0], entry_square[0], entry_total, clip
    )
    exit_master, exit_moment, exit_variance = adamw_step(
        exit_params[0], exit_mean[0], exit_square[0], exit_total, clip
    )
    entry_round = entry_master.astype(jnp.bfloat16)
    exit_round = exit_master.astype(jnp.bfloat16)
    entry_weights = lax.all_gather(entry_round, "group", axis=0, tiled=True)
    exit_weights = lax.all_gather(exit_round, "group", axis=0, tiled=True)
    return (
        entry_master[None],
        exit_master[None],
        entry_moment[None],
        exit_moment[None],
        entry_variance[None],
        exit_variance[None],
        entry_weights[None],
        exit_weights[None],
    )


def solution(mesh):
    placed = (
        P("group", "shard", None, None),
        P("group", "shard", None, None),
        P("shard", "group", None),
        P("shard", "group", None),
        P("shard", "group", None),
        P("shard", "group", None),
        P("shard", "group", None),
        P("shard", "group", None),
    )
    return jax.shard_map(
        body,
        mesh=mesh,
        in_specs=placed,
        out_specs=(
            P("shard", "group", None),
            P("shard", "group", None),
            P("shard", "group", None),
            P("shard", "group", None),
            P("shard", "group", None),
            P("shard", "group", None),
            P("shard", None, None),
            P("shard", None, None),
        ),
        check_vma=False,
    )
```

profile of v0, /device:TPU:2, one launch (start us, length us, event | category | flops | bytes accessed | tf_op | source)
XLA Modules:
  0.0 204.4 jit_solution(7940237761173604504)
XLA Ops:
  7.2 0.0 reduce-scatter.2.cloned.1.call-start
  7.2 3.2 %pad_maximum_fusion = f32[256,2304]{1,0:T(8,128)} fusion(f32[256,1024]{1,0:T(8,128)} %bitcast.67, f32[256,1280]{1,0:T(8,128)} %bitcast.65), kind=kLoop, calls=%fused_computation | loop fusion | flops 589824 | bytes 4718592 | tf_op jit(solution)/shard_map/concatenate | solution.py:47
  10.4 0.0 copy-start.4
  10.4 0.0 copy-start.5
  10.4 0.0 copy-start.6
  10.4 0.0 copy-start.1
  10.4 0.0 copy-start.2
  10.5 0.0 copy-start.3
  10.5 0.0 reduce-scatter.2.cloned.1.call-update
  10.5 78.5 %reduce-scatter.2.cloned.1.call-done = f32[16,2304]{1,0:T(8,128)} async-done(((f32[256,2304]{1,0:T(8,128)}), f32[16,2304]{1,0:T(8,128)}) %reduce-scatter.2.cloned.1.call-update) | async-done | bytes 147472 | tf_op jit(solution)/shard_map/reduce_scatter | solution.py:48
  89.0 0.0 copy-start
  89.0 1.1 mul.96
  90.1 0.1 reduce_sum.18
  90.2 0.1 broadcast_in_dim.27
  90.3 40.8 %all_to_all.5 = f32[512,1,128]{2,1,0:T(1,128)S(1)} all-to-all(f32[512,1,128]{2,1,0:T(1,128)S(1)} %broadcast_in_dim.27), channel_id=1, replica_groups=mesh['group'=16,'shard'=32] {'group','shard'}, dimensions={0} | all-to-all | bytes 524288 | tf_op jit(solution)/shard_map/all_to_all | solution.py:28
  131.1 0.7 reduce_sum.19
  132.5 0.0 copy-done.4
  132.5 0.0 copy-done.5
  132.5 0.0 copy-done.6
  132.5 1.5 fusion.10
  134.1 30.4 %all_gather.7 = bf16[256,1024]{1,0:T(8,128)(2,1)S(1)} all-gather(bf16[16,1024]{1,0:T(8,128)(2,1)S(1)} %get-tuple-element.8), channel_id=1, replica_groups=mesh['group'=16,'shard'=32] {'group'}, dimensions={0}, use_global_device_ids=true | all-gather | bytes 557056 | tf_op jit(solution)/shard_map/all_gather | solution.py:64
  164.5 0.0 copy-done.1
  164.5 0.0 copy-done.2
  164.5 0.0 copy-done.3
  164.5 0.0 copy-done
  164.5 0.7 fusion.11
  165.2 30.7 %all_gather.6 = bf16[256,1280]{1,0:T(8,128)(2,1)S(1)} all-gather(bf16[16,1280]{1,0:T(8,128)(2,1)S(1)} %get-tuple-element.10), channel_id=1, replica_groups=mesh['group'=16,'shard'=32] {'group'}, dimensions={0}, use_global_device_ids=true | all-gather | bytes 696320 | tf_op jit(solution)/shard_map/all_gather | solution.py:63
  195.9 0.8 copy.19
  196.8 0.8 copy.20
  (1 shorter events, 0.0 us)
Async XLA Ops:
  7.2 81.9 %reduce-scatter.2.cloned.1.call-start = ((), (), s32[]{:S(2)}) async-start(), calls=%async_computation.2 | async-start | bytes 2506752 | tf_op jit(solution)/shard_map/reduce_scatter | solution.py:48
  10.4 122.1 %copy-start.4 = (f32[1,16,1024]{2,1,0:T(8,128)S(1)}, f32[1,16,1024]{2,1,0:T(8,128)}, u32[]{:S(2)}) copy-start(f32[1,16,1024]{2,1,0:T(8,128)} %param.15) | copy-start | bytes 196612
  10.4 122.1 %copy-start.5 = (f32[1,16,1024]{2,1,0:T(8,128)S(1)}, f32[1,16,1024]{2,1,0:T(8,128)}, u32[]{:S(2)}) copy-start(f32[1,16,1024]{2,1,0:T(8,128)} %param.13) | copy-start | bytes 196612
  10.4 122.1 %copy-start.6 = (f32[1,16,1024]{2,1,0:T(8,128)S(1)}, f32[1,16,1024]{2,1,0:T(8,128)}, u32[]{:S(2)}) copy-start(f32[1,16,1024]{2,1,0:T(8,128)} %param.11) | copy-start | bytes 196612
  10.4 154.1 %copy-start.1 = (f32[1,16,1280]{2,1,0:T(8,128)S(1)}, f32[1,16,1280]{2,1,0:T(8,128)}, u32[]{:S(2)}) copy-start(f32[1,16,1280]{2,1,0:T(8,128)} %param.14) | copy-start | bytes 245764
  10.4 154.1 %copy-start.2 = (f32[1,16,1280]{2,1,0:T(8,128)S(1)}, f32[1,16,1280]{2,1,0:T(8,128)}, u32[]{:S(2)}) copy-start(f32[1,16,1280]{2,1,0:T(8,128)} %param.12) | copy-start | bytes 245764
  10.5 154.1 %copy-start.3 = (f32[1,16,1280]{2,1,0:T(8,128)S(1)}, f32[1,16,1280]{2,1,0:T(8,128)}, u32[]{:S(2)}) copy-start(f32[1,16,1280]{2,1,0:T(8,128)} %param.10) | copy-start | bytes 245764
  89.0 75.5 %copy-start = (f32[16,2304]{1,0:T(8,128)S(1)}, f32[16,2304]{1,0:T(8,128)}, u32[]{:S(2)}) copy-start(f32[16,2304]{1,0:T(8,128)} %reduce-scatter.2.cloned.1.call-done) | copy-start | bytes 442372
Sparse Core Ops, SparseCore 0:
  10.8 78.1 reduce-scatter.1
where the time goes:
time: 205 us; the launch traced here: 204 us
  blocking collectives  102 us (50%)
  waiting for transfers between devices  78.6 us (38%)
  between operations  14.8 us (7%)
  other arithmetic  7.27 us (4%)
    reduce_scatter x1, waiting for transfers between devices, body(): total = lax.psum_scatter(packed, 'group', scatter_dimension=0, tiled=True)  78.5 us
    all_to_all x1, blocking collectives, sum_everywhere(): return jnp.sum(lax.all_to_all(sent, axes, 0, 0))  40.8 us
    all_gather x1, blocking collectives, body(): entry_weights = lax.all_gather(entry_round, 'group', axis=0, tiled=True)  30.7 us
    all_gather x1, blocking collectives, body(): exit_weights = lax.all_gather(exit_round, 'group', axis=0, tiled=True)  30.4 us
  transfers between devices with their start and end apart: 1, of which 1 were waited for; matrix products, arithmetic and copies ran while one was open for 0% of the time, Pallas kernels for 0%

commit v1 on v0

--- a/solution.py
+++ b/solution.py
@@ -61,7 +61,25 @@
     entry_round = entry_master.astype(jnp.bfloat16)
     exit_round = exit_master.astype(jnp.bfloat16)
     entry_weights = lax.all_gather(entry_round, "group", axis=0, tiled=True)
-    exit_weights = lax.all_gather(exit_round, "group", axis=0, tiled=True)
+    length, here, span = (lax.axis_size("group"), lax.axis_index("group"), exit_round.shape[0])
+    right = [(i, (i + 1) % length) for i in range(length)]
+    left = [(i, (i - 1) % length) for i in range(length)]
+    exit_weights = jnp.zeros(
+        (*exit_round.shape[:0], length * span, *exit_round.shape[0 + 1 :]), exit_round.dtype
+    )
+    exit_weights = lax.dynamic_update_slice_in_dim(exit_weights, exit_round, here * span, axis=0)
+    from_left = from_right = exit_round
+    half = length // 2
+    for step in range(1, half + 1):
+        from_left = lax.ppermute(from_left, "group", right)
+        exit_weights = lax.dynamic_update_slice_in_dim(
+            exit_weights, from_left, (here - step) % length * span, axis=0
+        )
+        if step < length - half:
+            from_right = lax.ppermute(from_right, "group", left)
+            exit_weights = lax.dynamic_update_slice_in_dim(
+                exit_weights, from_right, (here + step) % length * span, axis=0
+            )
     return (
         entry_master[None],
         exit_master[None],

time: 205 us -> 231 us (1.13)
  the two profiles are of different devices: /device:TPU:2 before, /device:TPU:8 now
where the time goes in v1:
time: 231 us
  waiting for transfers between devices  107 us (46%)
  starting transfers between devices  68.1 us (29%)
  blocking collectives  30.3 us (13%)
  between operations  15.5 us (7%)
  other arithmetic  7.13 us (3%)
    reduce_scatter x1, waiting for transfers between devices, body(): total = lax.psum_scatter(packed, 'group', scatter_dimension=0, tiled=True)  78.6 us
    ppermute x7, starting transfers between devices, body(): from_right = lax.ppermute(from_right, 'group', left)  33.7 us
    all_gather x1, blocking collectives, body(): entry_weights = lax.all_gather(entry_round, 'group', axis=0, tiled=True)  30.3 us
    all_to_all x1, waiting for transfers between devices, sum_everywhere(): return jnp.sum(lax.all_to_all(sent, axes, 0, 0))  23.6 us
    ppermute x8, starting transfers between devices, body(): from_left = lax.ppermute(from_left, 'group', right)  17.6 us
    all_to_all x1, starting transfers between devices, sum_everywhere(): return jnp.sum(lax.all_to_all(sent, axes, 0, 0))  16.8 us
    ppermute x8, waiting for transfers between devices, body(): from_left = lax.ppermute(from_left, 'group', right)  5.06 us
  transfers between devices with their start and end apart: 17, of which 3 were waited for; matrix products, arithmetic and copies ran while one was open for 1% of the time, Pallas kernels for 0%

profile of v1, /device:TPU:8, one launch (start us, length us, event | category | flops | bytes accessed | tf_op | source)
XLA Modules:
  0.0 230.5 jit_solution(14241081796049920748)
XLA Ops:
  7.2 0.0 reduce-scatter.2.cloned.1.call-start
  7.2 3.2 %pad_maximum_fusion = f32[256,2304]{1,0:T(8,128)} fusion(f32[256,1024]{1,0:T(8,128)} %bitcast.97, f32[256,1280]{1,0:T(8,128)} %bitcast.95), kind=kLoop, calls=%fused_computation | loop fusion | flops 589824 | bytes 4718592 | tf_op jit(solution)/shard_map/concatenate | solution.py:47
  10.5 0.0 copy-start.5
  10.5 0.0 copy-start.6
  10.5 0.0 reduce-scatter.2.cloned.1.call-update
  10.5 78.6 %reduce-scatter.2.cloned.1.call-done = f32[16,2304]{1,0:T(8,128)} async-done(((f32[256,2304]{1,0:T(8,128)}), f32[16,2304]{1,0:T(8,128)}) %reduce-scatter.2.cloned.1.call-update) | async-done | bytes 147472 | tf_op jit(solution)/shard_map/reduce_scatter | solution.py:48
  89.1 1.1 mul.144
  90.2 0.1 reduce_sum.18
  90.3 0.8 broadcast_in_dim.60
  91.1 16.8 %all-to-all-start = ((f32[512,1,128]{2,1,0:T(1,128)}), f32[512,1,128]{2,1,0:T(1,128)S(1)}, u32[]{:S(2)}, u32[]{:S(2)}) async-start(f32[512,1,128]{2,1,0:T(1,128)} %broadcast_in_dim.60), calls=%async_computation.1 | async-start | bytes 524288 | tf_op jit(solution)/shard_map/all_to_all | solution.py:28
  108.3 23.6 %all-to-all-done = f32[512,1,128]{2,1,0:T(1,128)S(1)} async-done(((f32[512,1,128]{2,1,0:T(1,128)}), f32[512,1,128]{2,1,0:T(1,128)S(1)}, u32[]{:S(2)}, u32[]{:S(2)}) %all-to-all-start) | async-done | bytes 262176 | tf_op jit(solution)/shard_map/all_to_all | solution.py:28
  131.9 0.7 reduce_sum.19
  133.3 0.1 broadcast_in_dim.68
  133.4 0.7 bitcast_dynamic-update-slice_fusion.15
  134.1 2.8 %collective-permute-start = (bf16[16,1024]{1,0:T(8,128)(2,1)S(1)}, bf16[16,1024]{1,0:T(8,128)(2,1)S(1)}, u32[]{:S(2)}, u32[]{:S(2)}) collective-permute-start(bf16[16,1024]{1,0:T(8,128)(2,1)S(1)} %get-tuple-element.9), channel_id=1, source_target_pairs={{0,32},{32,64},{64,96},{96,128},{128,160},{160,192},{192,224},{224... | collective-permute-start | bytes 98312 | tf_op jit(solution)/shard_map/ppermute | solution.py:74
  136.9 4.3 %collective-permute-start.1 = (bf16[16,1024]{1,0:T(8,128)(2,1)S(1)}, bf16[16,1024]{1,0:T(8,128)(2,1)S(1)}, u32[]{:S(2)}, u32[]{:S(2)}) collective-permute-start(bf16[16,1024]{1,0:T(8,128)(2,1)S(1)} %get-tuple-element.9), channel_id=1, source_target_pairs={{0,480},{32,0},{64,32},{96,64},{128,96},{160,128},{192,160},{224,1... | collective-permute-start | bytes 98312 | tf_op jit(solution)/shard_map/ppermute | solution.py:79
  141.2 0.7 fusion.10
  141.9 30.3 %all_gather.3 = bf16[256,1280]{1,0:T(8,128)(2,1)S(1)} all-gather(bf16[16,1280]{1,0:T(8,128)(2,1)S(1)} %get-tuple-element.11), channel_id=1, replica_groups=mesh['group'=16,'shard'=32] {'group'}, dimensions={0}, use_global_device_ids=true | all-gather | bytes 696320 | tf_op jit(solution)/shard_map/all_gather | solution.py:63
  172.2 0.7 fusion.9
  172.9 0.0 collective-permute-done
  172.9 3.2 %collective-permute-start.2 = (bf16[16,1024]{1,0:T(8,128)(2,1)S(1)}, bf16[16,1024]{1,0:T(8,128)(2,1)S(1)}, u32[]{:S(2)}, u32[]{:S(2)}) collective-permute-start(bf16[16,1024]{1,0:T(8,128)(2,1)S(1)} %collective-permute-done), channel_id=1, source_target_pairs={{0,32},{32,64},{64,96},{96,128},{128,160},{160,192},{192,224},{224... | collective-permute-start | bytes 98312 | tf_op jit(solution)/shard_map/ppermute | solution.py:74
  176.1 0.0 collective-permute-done.1
  176.1 3.8 %collective-permute-start.3 = (bf16[16,1024]{1,0:T(8,128)(2,1)S(1)}, bf16[16,1024]{1,0:T(8,128)(2,1)S(1)}, u32[]{:S(2)}, u32[]{:S(2)}) collective-permute-start(bf16[16,1024]{1,0:T(8,128)(2,1)S(1)} %collective-permute-done.1), channel_id=1, source_target_pairs={{0,480},{32,0},{64,32},{96,64},{128,96},{160,128},{192,160},{224,1... | collective-permute-start | bytes 98312 | tf_op jit(solution)/shard_map/ppermute | solution.py:79
  180.0 0.0 collective-permute-done.2
  180.0 2.0 collective-permute-start.4
  182.0 0.0 collective-permute-done.3
  182.0 5.0 %collective-permute-start.5 = (bf16[16,1024]{1,0:T(8,128)(2,1)S(1)}, bf16[16,1024]{1,0:T(8,128)(2,1)S(1)}, u32[]{:S(2)}, u32[]{:S(2)}) collective-permute-start(bf16[16,1024]{1,0:T(8,128)(2,1)S(1)} %collective-permute-done.3), channel_id=1, source_target_pairs={{0,480},{32,0},{64,32},{96,64},{128,96},{160,128},{192,160},{224,1... | collective-permute-start | bytes 98312 | tf_op jit(solution)/shard_map/ppermute | solution.py:79
  187.1 0.0 collective-permute-done.4
  187.1 1.9 collective-permute-start.6
  189.1 0.0 collective-permute-done.5
  189.1 5.1 %collective-permute-start.7 = (bf16[16,1024]{1,0:T(8,128)(2,1)S(1)}, bf16[16,1024]{1,0:T(8,128)(2,1)S(1)}, u32[]{:S(2)}, u32[]{:S(2)}) collective-permute-start(bf16[16,1024]{1,0:T(8,128)(2,1)S(1)} %collective-permute-done.5), channel_id=1, source_target_pairs={{0,480},{32,0},{64,32},{96,64},{128,96},{160,128},{192,160},{224,1... | collective-permute-start | bytes 98312 | tf_op jit(solution)/shard_map/ppermute | solution.py:79
  194.2 0.0 collective-permute-done.6
  194.2 1.9 collective-permute-start.8
  196.2 0.0 collective-permute-done.7
  196.2 5.1 %collective-permute-start.9 = (bf16[16,1024]{1,0:T(8,128)(2,1)S(1)}, bf16[16,1024]{1,0:T(8,128)(2,1)S(1)}, u32[]{:S(2)}, u32[]{:S(2)}) collective-permute-start(bf16[16,1024]{1,0:T(8,128)(2,1)S(1)} %collective-permute-done.7), channel_id=1, source_target_pairs={{0,480},{32,0},{64,32},{96,64},{128,96},{160,128},{192,160},{224,1... | collective-permute-start | bytes 98312 | tf_op jit(solution)/shard_map/ppermute | solution.py:79
  201.4 0.0 collective-permute-done.8
  201.4 1.9 collective-permute-start.10
  203.3 0.0 collective-permute-done.9
  203.3 5.1 %collective-permute-start.11 = (bf16[16,1024]{1,0:T(8,128)(2,1)S(1)}, bf16[16,1024]{1,0:T(8,128)(2,1)S(1)}, u32[]{:S(2)}, u32[]{:S(2)}) collective-permute-start(bf16[16,1024]{1,0:T(8,128)(2,1)S(1)} %collective-permute-done.9), channel_id=1, source_target_pairs={{0,480},{32,0},{64,32},{96,64},{128,96},{160,128},{192,160},{224,1... | collective-permute-start | bytes 98312 | tf_op jit(solution)/shard_map/ppermute | solution.py:79
  208.5 1.9 collective-permute-start.12
  210.4 0.0 collective-permute-done.11
  210.4 5.1 %collective-permute-start.13 = (bf16[16,1024]{1,0:T(8,128)(2,1)S(1)}, bf16[16,1024]{1,0:T(8,128)(2,1)S(1)}, u32[]{:S(2)}, u32[]{:S(2)}) collective-permute-start(bf16[16,1024]{1,0:T(8,128)(2,1)S(1)} %collective-permute-done.11), channel_id=1, source_target_pairs={{0,480},{32,0},{64,32},{96,64},{128,96},{160,128},{192,160},{224,1... | collective-permute-start | bytes 98312 | tf_op jit(solution)/shard_map/ppermute | solution.py:79
  215.6 0.0 collective-permute-done.12
  215.6 1.9 collective-permute-start.14
  217.6 0.0 collective-permute-done.13
  217.6 5.0 %collective-permute-done.14 = bf16[16,1024]{1,0:T(8,128)(2,1)S(1)} collective-permute-done((bf16[16,1024]{1,0:T(8,128)(2,1)S(1)}, bf16[16,1024]{1,0:T(8,128)(2,1)S(1)}, u32[]{:S(2)}, u32[]{:S(2)}) %collective-permute-start.14) | collective-permute-done | bytes 32800 | tf_op jit(solution)/shard_map/ppermute | solution.py:74
  222.7 0.9 copy.34
  223.5 0.1 copy-done.1
  (30 shorter events, 0.2 us)
Async XLA Ops:
  7.2 82.0 %reduce-scatter.2.cloned.1.call-start = ((), (), s32[]{:S(2)}) async-start(), calls=%async_computation.2 | async-start | bytes 2506752 | tf_op jit(solution)/shard_map/reduce_scatter | solution.py:48
  10.4 122.9 %copy-start.2 = (f32[1,16,1024]{2,1,0:T(8,128)S(1)}, f32[1,16,1024]{2,1,0:T(8,128)}, u32[]{:S(2)}) copy-start(f32[1,16,1024]{2,1,0:T(8,128)} %param.15) | copy-start | bytes 196612
  10.5 122.9 %copy-start.3 = (f32[1,16,1024]{2,1,0:T(8,128)S(1)}, f32[1,16,1024]{2,1,0:T(8,128)}, u32[]{:S(2)}) copy-start(f32[1,16,1024]{2,1,0:T(8,128)} %param.13) | copy-start | bytes 196612
  10.5 122.9 %copy-start.7 = (f32[1,16,1024]{2,1,0:T(8,128)S(1)}, f32[1,16,1024]{2,1,0:T(8,128)}, u32[]{:S(2)}) copy-start(f32[1,16,1024]{2,1,0:T(8,128)} %param.11) | copy-start | bytes 196612
  10.5 130.7 %copy-start.4 = (f32[1,16,1280]{2,1,0:T(8,128)S(1)}, f32[1,16,1280]{2,1,0:T(8,128)}, u32[]{:S(2)}) copy-start(f32[1,16,1280]{2,1,0:T(8,128)} %param.14) | copy-start | bytes 245764
  10.5 130.7 %copy-start.5 = (f32[1,16,1280]{2,1,0:T(8,128)S(1)}, f32[1,16,1280]{2,1,0:T(8,128)}, u32[]{:S(2)}) copy-start(f32[1,16,1280]{2,1,0:T(8,128)} %param.12) | copy-start | bytes 245764
  10.5 130.7 %copy-start.6 = (f32[1,16,1280]{2,1,0:T(8,128)S(1)}, f32[1,16,1280]{2,1,0:T(8,128)}, u32[]{:S(2)}) copy-start(f32[1,16,1280]{2,1,0:T(8,128)} %param.10) | copy-start | bytes 245764
  89.1 44.2 %copy-start = (f32[16,2304]{1,0:T(8,128)S(1)}, f32[16,2304]{1,0:T(8,128)}, u32[]{:S(2)}) copy-start(f32[16,2304]{1,0:T(8,128)} %reduce-scatter.2.cloned.1.call-done) | copy-start | bytes 442372
  91.1 40.8 %all-to-all-start = ((f32[512,1,128]{2,1,0:T(1,128)}), f32[512,1,128]{2,1,0:T(1,128)S(1)}, u32[]{:S(2)}, u32[]{:S(2)}) async-start(f32[512,1,128]{2,1,0:T(1,128)} %broadcast_in_dim.60), calls=%async_computation.1 | async-start | bytes 524288 | tf_op jit(solution)/shard_map/all_to_all | solution.py:28
  134.1 38.8 %collective-permute-start = (bf16[16,1024]{1,0:T(8,128)(2,1)S(1)}, bf16[16,1024]{1,0:T(8,128)(2,1)S(1)}, u32[]{:S(2)}, u32[]{:S(2)}) collective-permute-start(bf16[16,1024]{1,0:T(8,128)(2,1)S(1)} %get-tuple-element.9), channel_id=1, source_target_pairs={{0,32},{32,64},{64,96},{96,128},{128,160},{160,192},{192,224},{224... | collective-permute-start | bytes 98312 | tf_op jit(solution)/shard_map/ppermute | solution.py:74
  136.9 39.2 %collective-permute-start.1 = (bf16[16,1024]{1,0:T(8,128)(2,1)S(1)}, bf16[16,1024]{1,0:T(8,128)(2,1)S(1)}, u32[]{:S(2)}, u32[]{:S(2)}) collective-permute-start(bf16[16,1024]{1,0:T(8,128)(2,1)S(1)} %get-tuple-element.9), channel_id=1, source_target_pairs={{0,480},{32,0},{64,32},{96,64},{128,96},{160,128},{192,160},{224,1... | collective-permute-start | bytes 98312 | tf_op jit(solution)/shard_map/ppermute | solution.py:79
  172.9 7.1 %collective-permute-start.2 = (bf16[16,1024]{1,0:T(8,128)(2,1)S(1)}, bf16[16,1024]{1,0:T(8,128)(2,1)S(1)}, u32[]{:S(2)}, u32[]{:S(2)}) collective-permute-start(bf16[16,1024]{1,0:T(8,128)(2,1)S(1)} %collective-permute-done), channel_id=1, source_target_pairs={{0,32},{32,64},{64,96},{96,128},{128,160},{160,192},{192,224},{224... | collective-permute-start | bytes 98312 | tf_op jit(solution)/shard_map/ppermute | solution.py:74
  176.1 5.9 %collective-permute-start.3 = (bf16[16,1024]{1,0:T(8,128)(2,1)S(1)}, bf16[16,1024]{1,0:T(8,128)(2,1)S(1)}, u32[]{:S(2)}, u32[]{:S(2)}) collective-permute-start(bf16[16,1024]{1,0:T(8,128)(2,1)S(1)} %collective-permute-done.1), channel_id=1, source_target_pairs={{0,480},{32,0},{64,32},{96,64},{128,96},{160,128},{192,160},{224,1... | collective-permute-start | bytes 98312 | tf_op jit(solution)/shard_map/ppermute | solution.py:79
  180.0 7.1 %collective-permute-start.4 = (bf16[16,1024]{1,0:T(8,128)(2,1)S(1)}, bf16[16,1024]{1,0:T(8,128)(2,1)S(1)}, u32[]{:S(2)}, u32[]{:S(2)}) collective-permute-start(bf16[16,1024]{1,0:T(8,128)(2,1)S(1)} %collective-permute-done.2), channel_id=1, source_target_pairs={{0,32},{32,64},{64,96},{96,128},{128,160},{160,192},{192,224},{224... | collective-permute-start | bytes 98312 | tf_op jit(solution)/shard_map/ppermute | solution.py:74
  182.0 7.0 %collective-permute-start.5 = (bf16[16,1024]{1,0:T(8,128)(2,1)S(1)}, bf16[16,1024]{1,0:T(8,128)(2,1)S(1)}, u32[]{:S(2)}, u32[]{:S(2)}) collective-permute-start(bf16[16,1024]{1,0:T(8,128)(2,1)S(1)} %collective-permute-done.3), channel_id=1, source_target_pairs={{0,480},{32,0},{64,32},{96,64},{128,96},{160,128},{192,160},{224,1... | collective-permute-start | bytes 98312 | tf_op jit(solution)/shard_map/ppermute | solution.py:79
  187.1 7.1 %collective-permute-start.6 = (bf16[16,1024]{1,0:T(8,128)(2,1)S(1)}, bf16[16,1024]{1,0:T(8,128)(2,1)S(1)}, u32[]{:S(2)}, u32[]{:S(2)}) collective-permute-start(bf16[16,1024]{1,0:T(8,128)(2,1)S(1)} %collective-permute-done.4), channel_id=1, source_target_pairs={{0,32},{32,64},{64,96},{96,128},{128,160},{160,192},{192,224},{224... | collective-permute-start | bytes 98312 | tf_op jit(solution)/shard_map/ppermute | solution.py:74
  189.1 7.1 %collective-permute-start.7 = (bf16[16,1024]{1,0:T(8,128)(2,1)S(1)}, bf16[16,1024]{1,0:T(8,128)(2,1)S(1)}, u32[]{:S(2)}, u32[]{:S(2)}) collective-permute-start(bf16[16,1024]{1,0:T(8,128)(2,1)S(1)} %collective-permute-done.5), channel_id=1, source_target_pairs={{0,480},{32,0},{64,32},{96,64},{128,96},{160,128},{192,160},{224,1... | collective-permute-start | bytes 98312 | tf_op jit(solution)/shard_map/ppermute | solution.py:79
  194.2 7.1 %collective-permute-start.8 = (bf16[16,1024]{1,0:T(8,128)(2,1)S(1)}, bf16[16,1024]{1,0:T(8,128)(2,1)S(1)}, u32[]{:S(2)}, u32[]{:S(2)}) collective-permute-start(bf16[16,1024]{1,0:T(8,128)(2,1)S(1)} %collective-permute-done.6), channel_id=1, source_target_pairs={{0,32},{32,64},{64,96},{96,128},{128,160},{160,192},{192,224},{224... | collective-permute-start | bytes 98312 | tf_op jit(solution)/shard_map/ppermute | solution.py:74
  196.2 7.1 %collective-permute-start.9 = (bf16[16,1024]{1,0:T(8,128)(2,1)S(1)}, bf16[16,1024]{1,0:T(8,128)(2,1)S(1)}, u32[]{:S(2)}, u32[]{:S(2)}) collective-permute-start(bf16[16,1024]{1,0:T(8,128)(2,1)S(1)} %collective-permute-done.7), channel_id=1, source_target_pairs={{0,480},{32,0},{64,32},{96,64},{128,96},{160,128},{192,160},{224,1... | collective-permute-start | bytes 98312 | tf_op jit(solution)/shard_map/ppermute | solution.py:79
  201.4 7.1 %collective-permute-start.10 = (bf16[16,1024]{1,0:T(8,128)(2,1)S(1)}, bf16[16,1024]{1,0:T(8,128)(2,1)S(1)}, u32[]{:S(2)}, u32[]{:S(2)}) collective-permute-start(bf16[16,1024]{1,0:T(8,128)(2,1)S(1)} %collective-permute-done.8), channel_id=1, source_target_pairs={{0,32},{32,64},{64,96},{96,128},{128,160},{160,192},{192,224},{224... | collective-permute-start | bytes 98312 | tf_op jit(solution)/shard_map/ppermute | solution.py:74
  203.3 7.1 %collective-permute-start.11 = (bf16[16,1024]{1,0:T(8,128)(2,1)S(1)}, bf16[16,1024]{1,0:T(8,128)(2,1)S(1)}, u32[]{:S(2)}, u32[]{:S(2)}) collective-permute-start(bf16[16,1024]{1,0:T(8,128)(2,1)S(1)} %collective-permute-done.9), channel_id=1, source_target_pairs={{0,480},{32,0},{64,32},{96,64},{128,96},{160,128},{192,160},{224,1... | collective-permute-start | bytes 98312 | tf_op jit(solution)/shard_map/ppermute | solution.py:79
  208.5 7.1 %collective-permute-start.12 = (bf16[16,1024]{1,0:T(8,128)(2,1)S(1)}, bf16[16,1024]{1,0:T(8,128)(2,1)S(1)}, u32[]{:S(2)}, u32[]{:S(2)}) collective-permute-start(bf16[16,1024]{1,0:T(8,128)(2,1)S(1)} %collective-permute-done.10), channel_id=1, source_target_pairs={{0,32},{32,64},{64,96},{96,128},{128,160},{160,192},{192,224},{224... | collective-permute-start | bytes 98312 | tf_op jit(solution)/shard_map/ppermute | solution.py:74
  210.4 7.1 %collective-permute-start.13 = (bf16[16,1024]{1,0:T(8,128)(2,1)S(1)}, bf16[16,1024]{1,0:T(8,128)(2,1)S(1)}, u32[]{:S(2)}, u32[]{:S(2)}) collective-permute-start(bf16[16,1024]{1,0:T(8,128)(2,1)S(1)} %collective-permute-done.11), channel_id=1, source_target_pairs={{0,480},{32,0},{64,32},{96,64},{128,96},{160,128},{192,160},{224,1... | collective-permute-start | bytes 98312 | tf_op jit(solution)/shard_map/ppermute | solution.py:79
  215.6 7.0 %collective-permute-start.14 = (bf16[16,1024]{1,0:T(8,128)(2,1)S(1)}, bf16[16,1024]{1,0:T(8,128)(2,1)S(1)}, u32[]{:S(2)}, u32[]{:S(2)}) collective-permute-start(bf16[16,1024]{1,0:T(8,128)(2,1)S(1)} %collective-permute-done.12), channel_id=1, source_target_pairs={{0,32},{32,64},{64,96},{96,128},{128,160},{160,192},{192,224},{224... | collective-permute-start | bytes 98312 | tf_op jit(solution)/shard_map/ppermute | solution.py:74
  222.6 1.0 copy-start.1
Sparse Core Ops, SparseCore 0:
  10.8 78.2 reduce-scatter.1
